TPU v7x, 32 devices: a whole 2x2x4 slice. The times are simulated.
32 devices in a mesh: dp: 8 (over y, x, core), seq: 4 (over z).
Axes of the slice: x: 2, y: 2, z: 4, core: 2. Of those that a mesh axis runs over, the one named last changes fastest.
Arguments:
- query: bfloat16 [8, 512, 512], P('dp', 'seq'), may hold values from -8 to 8
- key: bfloat16 [8, 512, 512], P('dp', 'seq'), may hold values from -8 to 8
- value: bfloat16 [8, 512, 512], P('dp', 'seq'), may hold values from -6 to 6
- out_ctx: bfloat16 [8, 512, 512], P('dp', 'seq'), may hold values from -6 to 6
- d_out: bfloat16 [8, 512, 512], P('dp', 'seq'), may hold values from -6 to 6
- score_bias: float32 [4, 4], P('seq'), may hold values from -2 to 2
- block_list: int32 [4, 4, 4], P('seq'), may hold values from 0 to 3, as said below
- block_count: int32 [4, 4], P('seq'), may hold values from 1 to 4, as said below
- hit_count: int32 [8], P('dp'), may hold values from 128 to 512, as said below
Outputs:
- d_query: bfloat16 [8, 512, 512], P('dp', 'seq')
- d_key: bfloat16 [8, 512, 512], P('dp', 'seq')
- d_value: bfloat16 [8, 512, 512], P('dp', 'seq')
- d_bias: float32 [4, 4], P('seq')
Inputs may be any that keep to these rules, and one draw needn't show every extreme that they name: Each list block_list[h, q] holds 4 different key blocks, the first being block q itself; only its first block_count[h, q] entries are used. `block_count`: some head has a list with all 4 entries used. `hit_count`: some event has all 512 hits real.
All inputs are finite; a program needn't handle non-finite values.
Results may differ from a plain program's by a relative error of at most 0.0049.
Values may be sent and summed in bfloat16 or wider, within the bound.
A program may use at most 64 MiB of HBM per device.

v0:
```python
import math

import jax
import jax.numpy as jnp
from jax import lax
from jax.sharding import PartitionSpec as P

MASKED = -1000000000.0


def head_grads(
    query_head,
    key_head,
    value_head,
    grad_head,
    delta_head,
    bias_row,
    list_rows,
    count_row,
    hit_limit,
    slot_end,
):
    nblocks = list_rows.shape[0]
    hits, head_dim = query_head.shape
    block = hits // nblocks
    scale = 1.0 / math.sqrt(head_dim)
    query_blocks = query_head.reshape(nblocks, block, head_dim)
    key_blocks = key_head.reshape(nblocks, block, head_dim)
    value_blocks = value_head.reshape(nblocks, block, head_dim)
    grad_blocks = grad_head.reshape(nblocks, block, head_dim)
    delta_blocks = delta_head.reshape(nblocks, block)
    within = jnp.arange(block, dtype=jnp.int32)
    block_ids = jnp.arange(nblocks, dtype=jnp.int32)
    row_valid = (jnp.arange(hits, dtype=jnp.int32) < hit_limit).reshape(nblocks, block)

    def slot_scores(slot_at):
        chosen = lax.dynamic_index_in_dim(list_rows, slot_at, axis=1, keepdims=False)
        key_taken = jnp.take(key_blocks, chosen, axis=0)
        matched = chosen[:, None] == block_ids[None, :]
        shift = jnp.sum(jnp.where(matched, bias_row[None, :], 0.0), axis=1)
        scores = (
            jnp.einsum("qid,qjd->qij", query_blocks, key_taken, preferred_element_type=jnp.float32)
            * scale
        )
        scores = scores + shift[:, None, None]
        key_real = chosen[:, None] * block + within[None, :] < hit_limit
        allowed = (slot_at < count_row)[:, None, None] & key_real[:, None, :]
        return (jnp.where(allowed, scores, MASKED), allowed, chosen, matched, key_taken)

    def first_pass(slot_at, state_now):
        row_top, row_total = state_now
        scores = slot_scores(slot_at)[0]
        new_top = jnp.maximum(row_top, jnp.max(scores, axis=2))
        row_total = row_total * jnp.exp(row_top - new_top) + jnp.sum(
            jnp.exp(scores - new_top[:, :, None]), axis=2
        )
        return (new_top, row_total)

    start_top = jnp.full((nblocks, block), -1e30, jnp.float32)
    start_total = jnp.zeros((nblocks, block), jnp.float32)
    row_top, row_total = lax.fori_loop(0, slot_end, first_pass, (start_top, start_total))
    lse = row_top + jnp.log(row_total)

    def second_pass(slot_at, state_now):
        grad_query, grad_key, grad_value, grad_bias = state_now
        scores, allowed, chosen, matched, key_taken = slot_scores(slot_at)
        value_taken = jnp.take(value_blocks, chosen, axis=0)
        probs = jnp.where(allowed & row_valid[:, :, None], jnp.exp(scores - lse[:, :, None]), 0.0)
        dprobs = jnp.einsum(
            "qid,qjd->qij", grad_blocks, value_taken, preferred_element_type=jnp.float32
        )
        dscores = probs * (dprobs - delta_blocks[:, :, None])
        probs_half = probs.astype(jnp.bfloat16)
        dscores_half = dscores.astype(jnp.bfloat16)
        grad_query = grad_query + jnp.einsum(
            "qij,qjd->qid", dscores_half, key_taken, preferred_element_type=jnp.float32
        )
        key_terms = jnp.einsum(
            "qij,qid->qjd", dscores_half, query_blocks, preferred_element_type=jnp.float32
        )
        value_terms = jnp.einsum(
            "qij,qid->qjd", probs_half, grad_blocks, preferred_element_type=jnp.float32
        )
        grad_key = grad_key.at[chosen].add(key_terms)
        grad_value = grad_value.at[chosen].add(value_terms)
        block_sums = jnp.sum(dscores, axis=(1, 2))
        grad_bias = grad_bias + jnp.sum(jnp.where(matched, block_sums[:, None], 0.0), axis=0)
        return (grad_query, grad_key, grad_value, grad_bias)

    zero_field = jnp.zeros((nblocks, block, head_dim), jnp.float32)
    start_state = (zero_field, zero_field, zero_field, jnp.zeros((nblocks,), jnp.float32))
    grad_query, grad_key, grad_value, grad_bias = lax.fori_loop(
        0, slot_end, second_pass, start_state
    )
    grad_query = (grad_query * scale).reshape(hits, head_dim).astype(jnp.bfloat16)
    grad_key = (grad_key * scale).reshape(hits, head_dim).astype(jnp.bfloat16)
    grad_value = grad_value.reshape(hits, head_dim).astype(jnp.bfloat16)
    return (grad_query, grad_key, grad_value, grad_bias)


def on_device(query, key, value, out_ctx, d_out, score_bias, block_list, block_count, hit_count):
    groups = lax.axis_size("seq")
    tok_rows = query.shape[1]
    width = query.shape[2]
    heads_here = score_bias.shape[0]
    heads_all = heads_here * groups
    head_dim = width // heads_all
    first_row = lax.axis_index("seq") * tok_rows
    hit_limit = hit_count[0]
    row_valid = first_row + jnp.arange(tok_rows, dtype=jnp.int32) < hit_limit
    grad_kept = jnp.where(row_valid[:, None], d_out[0], jnp.zeros((), jnp.bfloat16))

    def split_heads(field):
        return field.reshape(tok_rows, heads_all, head_dim)

    query_heads, key_heads, value_heads, out_heads, grad_heads = (
        lax.all_to_all(split_heads(query[0]), "seq", split_axis=1, concat_axis=0, tiled=True),
        lax.all_to_all(split_heads(key[0]), "seq", split_axis=1, concat_axis=0, tiled=True),
        lax.all_to_all(split_heads(value[0]), "seq", split_axis=1, concat_axis=0, tiled=True),
        lax.all_to_all(split_heads(out_ctx[0]), "seq", split_axis=1, concat_axis=0, tiled=True),
        lax.all_to_all(split_heads(grad_kept), "seq", split_axis=1, concat_axis=0, tiled=True),
    )
    delta_heads = jnp.sum(grad_heads.astype(jnp.float32) * out_heads.astype(jnp.float32), axis=2)
    count_row = block_count[0]
    grad_query, grad_key, grad_value, grad_bias = head_grads(
        query_heads[:, 0],
        key_heads[:, 0],
        value_heads[:, 0],
        grad_heads[:, 0],
        delta_heads[:, 0],
        score_bias[0],
        block_list[0],
        count_row,
        hit_limit,
        block_list.shape[2],
    )
    query_grads = [grad_query]
    key_grads = [grad_key]
    value_grads = [grad_value]
    bias_grads = [grad_bias]
    query_back, key_back, value_back = (
        lax.all_to_all(
            jnp.stack(query_grads, axis=1), "seq", split_axis=0, concat_axis=1, tiled=True
        ),
        lax.all_to_all(
            jnp.stack(key_grads, axis=1), "seq", split_axis=0, concat_axis=1, tiled=True
        ),
        lax.all_to_all(
            jnp.stack(value_grads, axis=1), "seq", split_axis=0, concat_axis=1, tiled=True
        ),
    )
    bias_total = lax.psum(jnp.stack(bias_grads, axis=0), "dp")
    return (
        query_back.reshape(1, tok_rows, width),
        key_back.reshape(1, tok_rows, width),
        value_back.reshape(1, tok_rows, width),
        bias_total,
    )


def solution(mesh):
    placed = (
        P("dp", "seq", None),
        P("dp", "seq", None),
        P("dp", "seq", None),
        P("dp", "seq", None),
        P("dp", "seq", None),
        P("seq", None),
        P("seq", None, None),
        P("seq", None),
        P("dp"),
    )
    return jax.shard_map(
        on_device,
        mesh=mesh,
        in_specs=placed,
        out_specs=(
            P("dp", "seq", None),
            P("dp", "seq", None),
            P("dp", "seq", None),
            P("seq", None),
        ),
        check_vma=False,
    )
```

profile of v0, /device:TPU:0, one launch (start us, length us, event | category | flops | bytes accessed | tf_op | source)
XLA Modules:
  0.0 120.0 jit_solution(9918450063467983925)
XLA Ops:
  0.6 1.7 %copy.95 = bf16[1,128,512]{1,2,0:T(8,128)(2,1)} copy(bf16[1,128,512]{2,1,0:T(8,128)(2,1)} %param.15) | data formatting | bytes 262144 | tf_op args[0]
  2.3 6.5 %all-to-all-start.1 = ((bf16[128,4,128]{0,2,1:T(8,128)(2,1)}), bf16[128,4,128]{0,2,1:T(8,128)(2,1)S(1)}, u32[]{:S(2)}, u32[]{:S(2)}) async-start(bf16[128,4,128]{0,2,1:T(8,128)(2,1)} %bitcast.7), calls=%async_computation.1 | async-start | bytes 262144 | tf_op jit(solution)/shard_map/all_to_all | solution.py:117
  8.8 0.8 copy.94
  9.5 5.3 %all-to-all-done.1 = bf16[128,4,128]{0,2,1:T(8,128)(2,1)S(1)} async-done(((bf16[128,4,128]{0,2,1:T(8,128)(2,1)}), bf16[128,4,128]{0,2,1:T(8,128)(2,1)S(1)}, u32[]{:S(2)}, u32[]{:S(2)}) %all-to-all-start.1) | async-done | bytes 131104 | tf_op jit(solution)/shard_map/all_to_all | solution.py:117
  14.9 3.5 %all-to-all-start = ((bf16[128,4,128]{0,2,1:T(8,128)(2,1)}), bf16[128,4,128]{0,2,1:T(8,128)(2,1)S(1)}, u32[]{:S(2)}, u32[]{:S(2)}) async-start(bf16[128,4,128]{0,2,1:T(8,128)(2,1)} %bitcast.3), calls=%async_computation | async-start | bytes 262144 | tf_op jit(solution)/shard_map/all_to_all | solution.py:118
  19.1 0.8 copy.99
  20.0 0.8 copy.101
  21.1 3.1 %all-to-all-done = bf16[128,4,128]{0,2,1:T(8,128)(2,1)S(1)} async-done(((bf16[128,4,128]{0,2,1:T(8,128)(2,1)}), bf16[128,4,128]{0,2,1:T(8,128)(2,1)S(1)}, u32[]{:S(2)}, u32[]{:S(2)}) %all-to-all-start) | async-done | bytes 131104 | tf_op jit(solution)/shard_map/all_to_all | solution.py:118
  24.2 3.3 %all-to-all-start.2 = ((bf16[128,4,128]{0,2,1:T(8,128)(2,1)}), bf16[128,4,128]{0,2,1:T(8,128)(2,1)S(1)}, u32[]{:S(2)}, u32[]{:S(2)}) async-start(bf16[128,4,128]{0,2,1:T(8,128)(2,1)} %bitcast.15), calls=%async_computation.2 | async-start | bytes 262144 | tf_op jit(solution)/shard_map/all_to_all | solution.py:119
  28.5 4.9 %all-to-all-done.2 = bf16[128,4,128]{0,2,1:T(8,128)(2,1)S(1)} async-done(((bf16[128,4,128]{0,2,1:T(8,128)(2,1)}), bf16[128,4,128]{0,2,1:T(8,128)(2,1)S(1)}, u32[]{:S(2)}, u32[]{:S(2)}) %all-to-all-start.2) | async-done | bytes 131104 | tf_op jit(solution)/shard_map/all_to_all | solution.py:119
  33.4 3.3 %all-to-all-start.3 = ((bf16[128,4,128]{0,2,1:T(8,128)(2,1)}), bf16[128,4,128]{0,2,1:T(8,128)(2,1)S(1)}, u32[]{:S(2)}, u32[]{:S(2)}) async-start(bf16[128,4,128]{0,2,1:T(8,128)(2,1)} %broadcast_select_fusion.4), calls=%async_computation.3 | async-start | bytes 262144 | tf_op jit(solution)/shard_map/all_to_all | solution.py:121
  37.4 7.7 %while.38 = (s32[]{:T(128)}, f32[4,128]{1,0:T(4,128)S(1)}, f32[4,128]{1,0:T(4,128)S(1)}, s32[4]{0:T(128)S(1)}, s32[4,4]{0,1:T(4,128)S(1)}, /*index=5*/s32[]{:T(1...) while((s32[]{:T(128)}, f32[4,128]{1,0:T(4,128)S(1)}, ...), condition=%wide.region_4.6_spmd.clone, body=%wide.region_0.5_spmd.clone.sunk | while | flops 17241176 | bytes 1081720 | solution.py:61
  45.2 5.1 %all-to-all-start.4 = ((bf16[128,4,128]{0,2,1:T(8,128)(2,1)}), bf16[128,4,128]{0,2,1:T(8,128)(2,1)S(1)}, u32[]{:S(2)}, u32[]{:S(2)}) async-start(bf16[128,4,128]{0,2,1:T(8,128)(2,1)} %bitcast.24), calls=%async_computation.4 | async-start | bytes 262144 | tf_op jit(solution)/shard_map/all_to_all | solution.py:120
  50.5 5.8 %all-to-all-done.4 = bf16[128,4,128]{0,2,1:T(8,128)(2,1)S(1)} async-done(((bf16[128,4,128]{0,2,1:T(8,128)(2,1)}), bf16[128,4,128]{0,2,1:T(8,128)(2,1)S(1)}, u32[]{:S(2)}, u32[]{:S(2)}) %all-to-all-start.4) | async-done | bytes 131104 | tf_op jit(solution)/shard_map/all_to_all | solution.py:120
  56.3 23.8 %while.39 = (s32[]{:T(128)}, f32[4,128,128]{2,1,0:T(8,128)S(1)}, f32[4,128,128]{2,1,0:T(8,128)S(1)}, f32[4,128,128]{2,1,0:T(8,128)S(1)}, f32[4]{0:T(128)S(1)}, /...) while((s32[]{:T(128)}, f32[4,128,128]{2,1,0:T(8,128)S(1)}, ...), condition=%wide.region_12.14_spmd.clone.clone.clone, body=%wide.region_6.0_spmd.clone.clone.clone.sunk | while | flops 85068952 | bytes 5253752 | solution.py:92
  82.1 3.3 %all-to-all-start.7 = ((bf16[4,2,8192]{2,1,0:T(2,128)(2,1)}), bf16[4,2,8192]{2,1,0:T(2,128)(2,1)S(1)}, u32[]{:S(2)}, u32[]{:S(2)}) async-start(bf16[4,2,8192]{2,1,0:T(2,128)(2,1)} %reshape.270), calls=%async_computation.7 | async-start | bytes 262144 | tf_op jit(solution)/shard_map/all_to_all | solution.py:148
  86.9 4.5 %all-to-all-done.7 = bf16[4,2,8192]{2,1,0:T(2,128)(2,1)S(1)} async-done(((bf16[4,2,8192]{2,1,0:T(2,128)(2,1)}), bf16[4,2,8192]{2,1,0:T(2,128)(2,1)S(1)}, u32[]{:S(2)}, u32[]{:S(2)}) %all-to-all-start.7) | async-done | bytes 131104 | tf_op jit(solution)/shard_map/all_to_all | solution.py:148
  91.3 3.3 %all-to-all-start.6 = ((bf16[4,2,8192]{2,1,0:T(2,128)(2,1)}), bf16[4,2,8192]{2,1,0:T(2,128)(2,1)S(1)}, u32[]{:S(2)}, u32[]{:S(2)}) async-start(bf16[4,2,8192]{2,1,0:T(2,128)(2,1)} %reshape.268), calls=%async_computation.6 | async-start | bytes 262144 | tf_op jit(solution)/shard_map/all_to_all | solution.py:145
  96.0 4.6 %all-to-all-done.6 = bf16[4,2,8192]{2,1,0:T(2,128)(2,1)S(1)} async-done(((bf16[4,2,8192]{2,1,0:T(2,128)(2,1)}), bf16[4,2,8192]{2,1,0:T(2,128)(2,1)S(1)}, u32[]{:S(2)}, u32[]{:S(2)}) %all-to-all-start.6) | async-done | bytes 131104 | tf_op jit(solution)/shard_map/all_to_all | solution.py:145
  100.6 3.9 %all-to-all-start.5 = ((bf16[4,2,8192]{2,1,0:T(2,128)(2,1)}), bf16[4,2,8192]{2,1,0:T(2,128)(2,1)S(1)}, u32[]{:S(2)}, u32[]{:S(2)}) async-start(bf16[4,2,8192]{2,1,0:T(2,128)(2,1)} %reshape.266), calls=%async_computation.5 | async-start | bytes 262144 | tf_op jit(solution)/shard_map/all_to_all | solution.py:142
  104.5 12.3 %psum.7 = f32[1,4]{1,0:T(1,128)} all-reduce(f32[1,4]{1,0:T(1,128)S(1)} %bitcast.144), channel_id=1, replica_groups=mesh['dp'=8,'seq'=4] {'dp'}, use_global_device_ids=true, to_apply=%region_13.15 | all-reduce | flops 4 | bytes 32 | tf_op jit(solution)/shard_map/psum | solution.py:152
  117.1 0.8 copy.115
  118.2 0.8 copy.114
  119.2 0.8 copy.113
  (178 shorter events, 38.8 us)
Async XLA Ops:
  2.3 6.5 %copy-start = (bf16[1,128,512]{2,1,0:T(8,128)(2,1)S(1)}, bf16[1,128,512]{2,1,0:T(8,128)(2,1)}, u32[]{:S(2)}) copy-start(bf16[1,128,512]{2,1,0:T(8,128)(2,1)} %param.16) | copy-start | bytes 393220
  2.3 12.6 %all-to-all-start.1 = ((bf16[128,4,128]{0,2,1:T(8,128)(2,1)}), bf16[128,4,128]{0,2,1:T(8,128)(2,1)S(1)}, u32[]{:S(2)}, u32[]{:S(2)}) async-start(bf16[128,4,128]{0,2,1:T(8,128)(2,1)} %bitcast.7), calls=%async_computation.1 | async-start | bytes 262144 | tf_op jit(solution)/shard_map/all_to_all | solution.py:117
  14.8 4.3 %copy-start.1 = (bf16[1,128,512]{2,1,0:T(8,128)(2,1)S(1)}, bf16[1,128,512]{2,1,0:T(8,128)(2,1)}, u32[]{:S(2)}) copy-start(bf16[1,128,512]{2,1,0:T(8,128)(2,1)} %param.17) | copy-start | bytes 393220
  14.9 9.4 %all-to-all-start = ((bf16[128,4,128]{0,2,1:T(8,128)(2,1)}), bf16[128,4,128]{0,2,1:T(8,128)(2,1)S(1)}, u32[]{:S(2)}, u32[]{:S(2)}) async-start(bf16[128,4,128]{0,2,1:T(8,128)(2,1)} %bitcast.3), calls=%async_computation | async-start | bytes 262144 | tf_op jit(solution)/shard_map/all_to_all | solution.py:118
  18.4 0.7 copy-start.5
  19.1 0.9 copy-start.2
  20.0 0.9 copy-start.3
  24.2 9.2 %all-to-all-start.2 = ((bf16[128,4,128]{0,2,1:T(8,128)(2,1)}), bf16[128,4,128]{0,2,1:T(8,128)(2,1)S(1)}, u32[]{:S(2)}, u32[]{:S(2)}) async-start(bf16[128,4,128]{0,2,1:T(8,128)(2,1)} %bitcast.15), calls=%async_computation.2 | async-start | bytes 262144 | tf_op jit(solution)/shard_map/all_to_all | solution.py:119
  33.4 11.8 %all-to-all-start.3 = ((bf16[128,4,128]{0,2,1:T(8,128)(2,1)}), bf16[128,4,128]{0,2,1:T(8,128)(2,1)S(1)}, u32[]{:S(2)}, u32[]{:S(2)}) async-start(bf16[128,4,128]{0,2,1:T(8,128)(2,1)} %broadcast_select_fusion.4), calls=%async_computation.3 | async-start | bytes 262144 | tf_op jit(solution)/shard_map/all_to_all | solution.py:121
  36.8 0.7 copy-start.4
  36.8 0.7 copy-start.6
  45.2 11.0 %all-to-all-start.4 = ((bf16[128,4,128]{0,2,1:T(8,128)(2,1)}), bf16[128,4,128]{0,2,1:T(8,128)(2,1)S(1)}, u32[]{:S(2)}, u32[]{:S(2)}) async-start(bf16[128,4,128]{0,2,1:T(8,128)(2,1)} %bitcast.24), calls=%async_computation.4 | async-start | bytes 262144 | tf_op jit(solution)/shard_map/all_to_all | solution.py:120
  82.1 9.2 %all-to-all-start.7 = ((bf16[4,2,8192]{2,1,0:T(2,128)(2,1)}), bf16[4,2,8192]{2,1,0:T(2,128)(2,1)S(1)}, u32[]{:S(2)}, u32[]{:S(2)}) async-start(bf16[4,2,8192]{2,1,0:T(2,128)(2,1)} %reshape.270), calls=%async_computation.7 | async-start | bytes 262144 | tf_op jit(solution)/shard_map/all_to_all | solution.py:148
  91.3 9.3 %all-to-all-start.6 = ((bf16[4,2,8192]{2,1,0:T(2,128)(2,1)}), bf16[4,2,8192]{2,1,0:T(2,128)(2,1)S(1)}, u32[]{:S(2)}, u32[]{:S(2)}) async-start(bf16[4,2,8192]{2,1,0:T(2,128)(2,1)} %reshape.268), calls=%async_computation.6 | async-start | bytes 262144 | tf_op jit(solution)/shard_map/all_to_all | solution.py:145
  100.6 18.3 %all-to-all-start.5 = ((bf16[4,2,8192]{2,1,0:T(2,128)(2,1)}), bf16[4,2,8192]{2,1,0:T(2,128)(2,1)S(1)}, u32[]{:S(2)}, u32[]{:S(2)}) async-start(bf16[4,2,8192]{2,1,0:T(2,128)(2,1)} %reshape.266), calls=%async_computation.5 | async-start | bytes 262144 | tf_op jit(solution)/shard_map/all_to_all | solution.py:142
where the time goes:
time: 121 us; the launch traced here: 120 us
  starting transfers between devices  32.2 us (27%)
  waiting for transfers between devices  28.2 us (23%)
  other arithmetic  19.7 us (16%)
  local copies, waits for them, and re-layouts  18.3 us (15%)
  blocking collectives  12.3 us (10%)
  matrix products  7.08 us (6%)
  between operations  1.57 us (1%)
    psum x1, blocking collectives, on_device(): bias_total = lax.psum(jnp.stack(bias_grads, axis=0), 'dp')  12.3 us
    unnamed x36, local copies, waits for them, and re-layouts  10.5 us
    all_to_all x1, starting transfers between devices, on_device(): lax.all_to_all(split_heads(query[0]), 'seq', split_axis=1, concat_axis=0,...  6.48 us
    all_to_all x1, waiting for transfers between devices, on_device(): lax.all_to_all(split_heads(out_ctx[0]), 'seq', split_axis=1, concat_axis=...  5.77 us
    and x8, other arithmetic, slot_scores(): allowed = (slot_at < count_row)[:, None, None] & key_real[:, None, :]  5.77 us
    all_to_all x1, waiting for transfers between devices, on_device(): lax.all_to_all(split_heads(query[0]), 'seq', split_axis=1, concat_axis=0,...  5.31 us
    all_to_all x1, starting transfers between devices, on_device(): lax.all_to_all(split_heads(out_ctx[0]), 'seq', split_axis=1, concat_axis=...  5.07 us
    all_to_all x1, waiting for transfers between devices, on_device(): lax.all_to_all(split_heads(value[0]), 'seq', split_axis=1, concat_axis=0,...  4.94 us
  transfers between devices with their start and end apart: 8, of which 6 were waited for; matrix products, arithmetic and copies ran while one was open for 13% of the time, Pallas kernels for 0%

commit v1 on v0

v1 whole, which is shorter than its diff:
```python
import functools
import math

import jax
import jax.numpy as jnp
from jax import lax
from jax.experimental import pallas as pl
from jax.experimental.pallas import tpu as pltpu
from jax.sharding import PartitionSpec as P

MASKED = -1000000000.0
MESH = pl.DeviceIdType.MESH
KEY, QUERY, GRAD, VALUE, DELTA, DVALUE, DKEY, DQUERY = range(8)


def kernel(
    n,
    ndp,
    head_dim,
    q_hbm,
    k_hbm,
    v_hbm,
    o_hbm,
    g_hbm,
    bias_ref,
    list_ref,
    count_ref,
    hit_ref,
    dq_hbm,
    dk_hbm,
    dv_hbm,
    db_ref,
    kbuf,
    qbuf,
    gbuf,
    vbuf,
    delta_in,
    delta_out,
    g_own,
    o_own,
    probs,
    probs_half,
    ds_half,
    dv_out,
    dk_out,
    dq_out,
    bias_out,
    bias_in,
    send_sem,
    recv_sem,
    own_sem,
    bias_send,
    bias_recv,
):
    me = lax.axis_index("seq")
    here = lax.axis_index("dp")
    rows = q_hbm.shape[1]
    hits = n * rows
    slots = list_ref.shape[2]
    scale = 1.0 / math.sqrt(head_dim)
    above = n - 1 - me

    def peer_of(r):
        return jnp.where(r < above, n - 1 - r, r - above)

    def source_of(r):
        return me if r == 0 else peer_of(n - 1 - r)

    def lanes(h):
        return pl.ds(pl.multiple_of(h * head_dim, head_dim), head_dim)

    load_g = pltpu.make_async_copy(g_hbm.at[0], g_own, own_sem.at[DVALUE])
    load_o = pltpu.make_async_copy(o_hbm.at[0], o_own, own_sem.at[DKEY])
    load_g.start()
    load_o.start()
    sources = {KEY: k_hbm, QUERY: q_hbm, GRAD: g_hbm, VALUE: v_hbm}
    targets = {KEY: kbuf, QUERY: qbuf, GRAD: gbuf, VALUE: vbuf}
    own = {}
    for kind in (KEY, QUERY, GRAD, VALUE):
        own[kind] = pltpu.make_async_copy(
            sources[kind].at[0, :, lanes(me)], targets[kind].at[me], own_sem.at[kind]
        )
        own[kind].start()

    barrier = pltpu.get_barrier_semaphore()
    for r in range(n - 1):
        pl.semaphore_signal(barrier, inc=1, device_id={"seq": peer_of(r)}, device_id_type=MESH)
    for r in range(1, ndp):
        pl.semaphore_signal(
            barrier, inc=1, device_id={"dp": lax.rem(here + r, ndp)}, device_id_type=MESH
        )
    pl.semaphore_wait(barrier, n - 1 + ndp - 1)

    def out_copy(kind, peer):
        return pltpu.make_async_remote_copy(
            src_ref=sources[kind].at[0, :, lanes(peer)],
            dst_ref=targets[kind].at[me],
            send_sem=send_sem.at[kind, peer],
            recv_sem=recv_sem.at[kind, me],
            device_id={"seq": peer},
            device_id_type=MESH,
        )

    def wait_in(kind, buf, peer):
        pltpu.make_async_remote_copy(
            src_ref=buf,
            dst_ref=buf,
            send_sem=send_sem.at[kind, peer],
            recv_sem=recv_sem.at[kind, peer],
            device_id={"seq": peer},
            device_id_type=MESH,
        ).wait_recv()

    sent = []

    def send(copy):
        copy.start()
        sent.append(copy)

    for kind in (KEY, QUERY):
        for r in range(n - 1):
            send(out_copy(kind, peer_of(r)))

    load_g.wait()
    load_o.wait()
    for h in range(n):
        cols = slice(h * head_dim, (h + 1) * head_dim)
        product = g_own[:, cols].astype(jnp.float32) * o_own[:, cols].astype(jnp.float32)
        delta_out[h] = jnp.sum(product.T, axis=0, keepdims=True)
    for r in range(n - 1):
        peer = peer_of(r)
        send(
            pltpu.make_async_remote_copy(
                src_ref=delta_out.at[peer],
                dst_ref=delta_in.at[me],
                send_sem=send_sem.at[DELTA, peer],
                recv_sem=recv_sem.at[DELTA, me],
                device_id={"seq": peer},
                device_id_type=MESH,
            )
        )
    delta_in[me] = delta_out[me]
    for kind in (GRAD, VALUE):
        for r in range(n - 1):
            send(out_copy(kind, peer_of(r)))

    hit_limit = hit_ref[0]
    for kind in (KEY, QUERY):
        own[kind].wait()
        for r in range(n - 1):
            peer = peer_of(r)
            wait_in(kind, targets[kind].at[peer], peer)
    q_all = qbuf[...].reshape(hits, head_dim)
    lane = lax.broadcasted_iota(jnp.int32, (1, hits), 1)
    within = lax.broadcasted_iota(jnp.int32, (rows, 1), 0)

    def score_step(b, top):
        shift = jnp.full((1, hits), MASKED, jnp.float32)
        for qb in range(n):
            used = jnp.int32(0)
            for s in range(slots):
                hit = (list_ref[0, qb, s] == b) & (s < count_ref[0, qb])
                used = jnp.where(hit, jnp.int32(1), used)
            inside = (lane >= qb * rows) & (lane < (qb + 1) * rows)
            shift = jnp.where(inside & (used > 0), bias_ref[0, b], shift)
        real = jnp.where(b * rows + within < hit_limit, 0.0, MASKED)
        scores = (
            lax.dot_general(
                kbuf[b], q_all, (((1,), (1,)), ((), ())), preferred_element_type=jnp.float32
            )
            * scale
        )
        scores = (scores + shift) + real
        probs[b] = scores
        return jnp.maximum(top, jnp.max(scores, axis=0, keepdims=True))

    short = n <= 4
    top = lax.fori_loop(
        0, n, score_step, jnp.full((1, hits), -3e9, jnp.float32), unroll=short
    )

    def exp_step(b, total):
        raised = jnp.exp(probs[b] - top)
        probs[b] = raised
        return total + jnp.sum(raised, axis=0, keepdims=True)

    total = lax.fori_loop(0, n, exp_step, jnp.zeros((1, hits), jnp.float32), unroll=short)
    factor = jnp.where(lane < hit_limit, 1.0 / total, 0.0)

    def scale_step(b, carry):
        scaled = probs[b] * factor
        probs[b] = scaled
        probs_half[b] = scaled.astype(jnp.bfloat16)
        return carry

    lax.fori_loop(0, n, scale_step, 0, unroll=short)

    def back_copy(kind, buf, out, peer):
        return pltpu.make_async_remote_copy(
            src_ref=buf.at[peer],
            dst_ref=out.at[0, :, lanes(me)],
            send_sem=send_sem.at[kind, peer],
            recv_sem=recv_sem.at[kind, me],
            device_id={"seq": peer},
            device_id_type=MESH,
        )

    def keep_copy(kind, buf, out):
        copy = pltpu.make_async_copy(buf.at[me], out.at[0, :, lanes(me)], own_sem.at[kind])
        copy.start()
        return copy

    kept = []
    own[GRAD].wait()
    for r in range(n - 1):
        peer = peer_of(r)
        wait_in(GRAD, gbuf.at[peer], peer)
    g_all = gbuf[...].reshape(hits, head_dim)
    for r in range(n):
        b = peer_of(r) if r < n - 1 else me
        dv_out[b] = jnp.dot(probs_half[b], g_all, preferred_element_type=jnp.float32).astype(
            jnp.bfloat16
        )
        if r < n - 1:
            send(back_copy(DVALUE, dv_out, dv_hbm, b))
        else:
            kept.append(keep_copy(DVALUE, dv_out, dv_hbm))

    for r in range(n - 1):
        peer = peer_of(r)
        wait_in(DELTA, delta_in.at[peer], peer)
    delta = jnp.concatenate([delta_in[b] for b in range(n)], axis=1)
    spot = lax.broadcasted_iota(jnp.int32, bias_out.shape, 1)
    bias_sums = jnp.zeros(bias_out.shape, jnp.float32)
    own[VALUE].wait()
    for r in range(n):
        b = source_of(r)
        if r > 0:
            wait_in(VALUE, vbuf.at[b], b)
        dprobs = lax.dot_general(
            vbuf[b], g_all, (((1,), (1,)), ((), ())), preferred_element_type=jnp.float32
        )
        dscores = probs[b] * (dprobs - delta)
        half = dscores.astype(jnp.bfloat16)
        ds_half[b] = half
        grad = jnp.dot(half, q_all, preferred_element_type=jnp.float32)
        dk_out[b] = (grad * scale).astype(jnp.bfloat16)
        if r > 0:
            send(back_copy(DKEY, dk_out, dk_hbm, b))
        else:
            kept.append(keep_copy(DKEY, dk_out, dk_hbm))
        block_sum = jnp.sum(jnp.sum(dscores, axis=0, keepdims=True), axis=1, keepdims=True)
        bias_sums = bias_sums + jnp.where(spot == b, block_sum, 0.0)
    bias_out[...] = bias_sums
    bias_sent = []
    for r in range(1, ndp):
        copy = pltpu.make_async_remote_copy(
            src_ref=bias_out,
            dst_ref=bias_in.at[here],
            send_sem=bias_send.at[r],
            recv_sem=bias_recv.at[here],
            device_id={"dp": lax.rem(here + r, ndp)},
            device_id_type=MESH,
        )
        copy.start()
        bias_sent.append(copy)
    bias_in[here] = bias_sums

    k_all = kbuf[...].reshape(hits, head_dim)
    for r in range(n):
        b = peer_of(r) if r < n - 1 else me
        picked = ds_half[:, :, pl.ds(pl.multiple_of(b * rows, rows), rows)].reshape(hits, rows)
        grad = lax.dot_general(
            picked, k_all, (((0,), (0,)), ((), ())), preferred_element_type=jnp.float32
        )
        dq_out[b] = (grad * scale).astype(jnp.bfloat16)
        if r < n - 1:
            send(back_copy(DQUERY, dq_out, dq_hbm, b))
        else:
            kept.append(keep_copy(DQUERY, dq_out, dq_hbm))

    for r in range(1, ndp):
        other = lax.rem(here + r, ndp)
        pltpu.make_async_remote_copy(
            src_ref=bias_in.at[other],
            dst_ref=bias_in.at[other],
            send_sem=bias_send.at[r],
            recv_sem=bias_recv.at[other],
            device_id={"dp": other},
            device_id_type=MESH,
        ).wait_recv()
    db_ref[...] = jnp.sum(bias_in[...], axis=0)[:, : db_ref.shape[1]]

    for kind, out in ((DVALUE, dv_hbm), (DKEY, dk_hbm), (DQUERY, dq_hbm)):
        for r in range(n - 1):
            peer = peer_of(r)
            wait_in(kind, out.at[0, :, lanes(peer)], peer)
    for copy in sent + bias_sent:
        copy.wait_send()
    for copy in kept:
        copy.wait()


def on_device(query, key, value, out_ctx, d_out, score_bias, block_list, block_count, hit_count):
    n = lax.axis_size("seq")
    ndp = lax.axis_size("dp")
    _, rows, width = query.shape
    head_dim = width // (score_bias.shape[0] * n)
    assert score_bias.shape[0] == 1 and block_list.shape[1] == n
    hits = n * rows
    padded = -(-n // 128) * 128
    half, full = jnp.bfloat16, jnp.float32
    any_ref = pl.BlockSpec(memory_space=pl.ANY)
    smem = pl.BlockSpec(memory_space=pltpu.SMEM)
    field = jax.ShapeDtypeStruct(query.shape, query.dtype)
    return pl.pallas_call(
        functools.partial(kernel, n, ndp, head_dim),
        out_shape=(field, field, field, jax.ShapeDtypeStruct((1, n), full)),
        in_specs=[any_ref] * 5 + [smem] * 4,
        out_specs=(any_ref, any_ref, any_ref, pl.BlockSpec(memory_space=pltpu.VMEM)),
        scratch_shapes=[
            pltpu.VMEM((n, rows, head_dim), half),
            pltpu.VMEM((n, rows, head_dim), half),
            pltpu.VMEM((n, rows, head_dim), half),
            pltpu.VMEM((n, rows, head_dim), half),
            pltpu.VMEM((n, 1, rows), full),
            pltpu.VMEM((n, 1, rows), full),
            pltpu.VMEM((rows, width), half),
            pltpu.VMEM((rows, width), half),
            pltpu.VMEM((n, rows, hits), full),
            pltpu.VMEM((n, rows, hits), half),
            pltpu.VMEM((n, rows, hits), half),
            pltpu.VMEM((n, rows, head_dim), half),
            pltpu.VMEM((n, rows, head_dim), half),
            pltpu.VMEM((n, rows, head_dim), half),
            pltpu.VMEM((1, padded), full),
            pltpu.VMEM((ndp, 1, padded), full),
            pltpu.SemaphoreType.DMA((8, n)),
            pltpu.SemaphoreType.DMA((8, n)),
            pltpu.SemaphoreType.DMA((8,)),
            pltpu.SemaphoreType.DMA((ndp,)),
            pltpu.SemaphoreType.DMA((ndp,)),
        ],
        compiler_params=pltpu.CompilerParams(
            collective_id=0, has_side_effects=True, vmem_limit_bytes=60 * 1024 * 1024
        ),
    )(query, key, value, out_ctx, d_out, score_bias, block_list, block_count, hit_count)


def solution(mesh):
    placed = (
        P("dp", "seq", None),
        P("dp", "seq", None),
        P("dp", "seq", None),
        P("dp", "seq", None),
        P("dp", "seq", None),
        P("seq", None),
        P("seq", None, None),
        P("seq", None),
        P("dp"),
    )
    return jax.shard_map(
        on_device,
        mesh=mesh,
        in_specs=placed,
        out_specs=(
            P("dp", "seq", None),
            P("dp", "seq", None),
            P("dp", "seq", None),
            P("seq", None),
        ),
        check_vma=False,
    )
```

time: 121 us -> 34.6 us (0.29)
  starting transfers between devices: 32.2 us -> 0 us
  Pallas kernels: 0 us -> 29.4 us
  waiting for transfers between devices: 28.2 us -> 0 us
  other arithmetic: 19.7 us -> 0 us
  local copies, waits for them, and re-layouts: 18.3 us -> 3.73 us
  blocking collectives: 12.3 us -> 0 us
  matrix products: 7.08 us -> 0 us
    all_to_all x8 -> x0, starting transfers between devices: 32.2 us -> none  [the longest x1 6.48 us: on_device(): lax.all_to_all(split_heads(query[0]), 'seq', split_axis=1, concat_axis=0,...]
    pallas_call x0 -> x1, Pallas kernels: none -> 29.4 us  [on_device(): pl.pallas_call(functools.partial(kernel, n, ndp, head_dim), out_shape=(fi...]
    all_to_all x8 -> x0, waiting for transfers between devices: 28.2 us -> none  [the longest x1 5.77 us: on_device(): lax.all_to_all(split_heads(out_ctx[0]), 'seq', split_axis=1, concat_axis=...]
    psum x1 -> x0, blocking collectives: 12.3 us -> none  [on_device(): bias_total = lax.psum(jnp.stack(bias_grads, axis=0), 'dp')]
    and x20 -> x0, other arithmetic: 8.47 us -> none  [the longest x8 5.77 us: slot_scores(): allowed = (slot_at < count_row)[:, None, None] & key_real[:, None, :]]
    dot_general x24 -> x0, matrix products: 7.08 us -> none  [the longest x8 3.16 us: slot_scores(): jnp.einsum('qid,qjd->qij', query_blocks, key_taken, preferred_element_typ...]
    gather x12 -> x0, local copies, waits for them, and re-layouts: 6.87 us -> none  [the longest x8 4.58 us: slot_scores(): key_taken = jnp.take(key_blocks, chosen, axis=0)]
    unnamed x36 -> x10, local copies, waits for them, and re-layouts: 10.5 us -> 3.73 us
  transfers between devices with their start and end apart: 8 -> 0, of which waited for: 6 -> 0; matrix products, arithmetic and copies ran while one was open for 13% -> 0% of each run, Pallas kernels for 0% -> 0%
where the time goes in v1:
time: 34.6 us; the launch traced here: 34.4 us
  Pallas kernels  29.4 us (85%)
  local copies, waits for them, and re-layouts  3.73 us (11%)
  between operations  1.3 us (4%)
    pallas_call x1, Pallas kernels, on_device(): pl.pallas_call(functools.partial(kernel, n, ndp, head_dim), out_shape=(fi...  29.4 us
    unnamed x10, local copies, waits for them, and re-layouts  3.73 us

profile of v1, /device:TPU:0, one launch (start us, length us, event | category | flops | bytes accessed | tf_op | source)
XLA Modules:
  0.0 34.4 jit_solution(13296673433549245334)
XLA Ops:
  1.3 29.4 %shard_map.120 = (bf16[1,128,512]{2,1,0:T(8,128)(2,1)}, bf16[1,128,512]{2,1,0:T(8,128)(2,1)}, bf16[1,128,512]{2,1,0:T(8,128)(2,1)}, f32[1,4]{1,0:T(1,128)}) custom-call(bf16[1,128,512]{2,1,0:T(8,128)(2,1)} %q_hbm.1, bf16[1,128,512]{2,1,0:T(8,128)(2,1)} %k_hbm.1, bf16[1,128,512]{2,1,0:T(8,128)(2,1)} %v_hbm.1, bf16[1,128,512]{2,1,0:T(8,128)(2,1)} %o_hbm.1, ...), custom_call_target="tpu_custom_call" | custom-call | tf_op jit(solution)/shard_map/pallas_call | solution.py:316
  30.6 0.0 copy-start.1
  30.7 1.6 %copy.18 = bf16[1,128,512]{2,1,0:T(8,128)(2,1)} copy(bf16[1,128,512]{2,1,0:T(8,128)(2,1)} %get-tuple-element.8) | data formatting | bytes 262144
  32.3 0.0 copy-done.1
  32.3 0.0 copy-start
  32.3 0.7 %copy.19 = bf16[1,128,512]{2,1,0:T(8,128)(2,1)} copy(bf16[1,128,512]{2,1,0:T(8,128)(2,1)S(1)} %copy-done.1) | data formatting | bytes 262144
  32.9 0.3 copy-done
  33.2 0.0 copy-start.2
  33.2 0.7 %copy.20 = bf16[1,128,512]{2,1,0:T(8,128)(2,1)} copy(bf16[1,128,512]{2,1,0:T(8,128)(2,1)S(1)} %copy-done) | data formatting | bytes 262144
  33.9 0.0 copy-done.2
  33.9 0.5 %copy.21 = f32[1,4]{1,0:T(1,128)} copy(f32[1,4]{1,0:T(1,128)S(1)} %copy-done.2) | data formatting | bytes 32
Async XLA Ops:
  30.6 1.6 %copy-start.1 = (bf16[1,128,512]{2,1,0:T(8,128)(2,1)S(1)}, bf16[1,128,512]{2,1,0:T(8,128)(2,1)}, u32[]{:S(2)}) copy-start(bf16[1,128,512]{2,1,0:T(8,128)(2,1)} %get-tuple-element.9) | copy-start | bytes 393220
  32.3 1.0 %copy-start = (bf16[1,128,512]{2,1,0:T(8,128)(2,1)S(1)}, bf16[1,128,512]{2,1,0:T(8,128)(2,1)}, u32[]{:S(2)}) copy-start(bf16[1,128,512]{2,1,0:T(8,128)(2,1)} %get-tuple-element.10) | copy-start | bytes 393220
  33.2 0.7 %copy-start.2 = (f32[1,4]{1,0:T(1,128)S(1)}, f32[1,4]{1,0:T(1,128)}, u32[]{:S(2)}) copy-start(f32[1,4]{1,0:T(1,128)} %get-tuple-element.11) | copy-start | bytes 52

commit v2 on v1

--- a/solution.py
+++ b/solution.py
@@ -22,13 +22,13 @@
     v_hbm,
     o_hbm,
     g_hbm,
-    bias_ref,
-    list_ref,
-    count_ref,
-    hit_ref,
-    dq_hbm,
-    dk_hbm,
-    dv_hbm,
+    bias_hbm,
+    list_hbm,
+    count_hbm,
+    hit_hbm,
+    dq_ref,
+    dk_ref,
+    dv_ref,
     db_ref,
     kbuf,
     qbuf,
@@ -46,11 +46,16 @@
     dq_out,
     bias_out,
     bias_in,
+    bias_ref,
+    list_ref,
+    count_ref,
+    hit_ref,
     send_sem,
     recv_sem,
     own_sem,
     bias_send,
     bias_recv,
+    table_sem,
 ):
     me = lax.axis_index("seq")
     here = lax.axis_index("dp")
@@ -73,6 +78,14 @@
     load_o = pltpu.make_async_copy(o_hbm.at[0], o_own, own_sem.at[DKEY])
     load_g.start()
     load_o.start()
+    tables = [
+        pltpu.make_async_copy(src, dst, table_sem.at[i])
+        for i, (src, dst) in enumerate(
+            ((bias_hbm, bias_ref), (list_hbm, list_ref), (count_hbm, count_ref), (hit_hbm, hit_ref))
+        )
+    ]
+    for copy in tables:
+        copy.start()
     sources = {KEY: k_hbm, QUERY: q_hbm, GRAD: g_hbm, VALUE: v_hbm}
     targets = {KEY: kbuf, QUERY: qbuf, GRAD: gbuf, VALUE: vbuf}
     own = {}
@@ -144,6 +157,8 @@
         for r in range(n - 1):
             send(out_copy(kind, peer_of(r)))
 
+    for copy in tables:
+        copy.wait()
     hit_limit = hit_ref[0]
     for kind in (KEY, QUERY):
         own[kind].wait()
@@ -198,19 +213,13 @@
     def back_copy(kind, buf, out, peer):
         return pltpu.make_async_remote_copy(
             src_ref=buf.at[peer],
-            dst_ref=out.at[0, :, lanes(me)],
+            dst_ref=out.at[:, lanes(me)],
             send_sem=send_sem.at[kind, peer],
             recv_sem=recv_sem.at[kind, me],
             device_id={"seq": peer},
             device_id_type=MESH,
         )
 
-    def keep_copy(kind, buf, out):
-        copy = pltpu.make_async_copy(buf.at[me], out.at[0, :, lanes(me)], own_sem.at[kind])
-        copy.start()
-        return copy
-
-    kept = []
     own[GRAD].wait()
     for r in range(n - 1):
         peer = peer_of(r)
@@ -218,13 +227,12 @@
     g_all = gbuf[...].reshape(hits, head_dim)
     for r in range(n):
         b = peer_of(r) if r < n - 1 else me
-        dv_out[b] = jnp.dot(probs_half[b], g_all, preferred_element_type=jnp.float32).astype(
-            jnp.bfloat16
-        )
+        grad = jnp.dot(probs_half[b], g_all, preferred_element_type=jnp.float32)
         if r < n - 1:
-            send(back_copy(DVALUE, dv_out, dv_hbm, b))
+            dv_out[b] = grad.astype(jnp.bfloat16)
+            send(back_copy(DVALUE, dv_out, dv_ref, b))
         else:
-            kept.append(keep_copy(DVALUE, dv_out, dv_hbm))
+            dv_ref[:, lanes(me)] = grad.astype(jnp.bfloat16)
 
     for r in range(n - 1):
         peer = peer_of(r)
@@ -244,11 +252,11 @@
         half = dscores.astype(jnp.bfloat16)
         ds_half[b] = half
         grad = jnp.dot(half, q_all, preferred_element_type=jnp.float32)
-        dk_out[b] = (grad * scale).astype(jnp.bfloat16)
         if r > 0:
-            send(back_copy(DKEY, dk_out, dk_hbm, b))
+            dk_out[b] = (grad * scale).astype(jnp.bfloat16)
+            send(back_copy(DKEY, dk_out, dk_ref, b))
         else:
-            kept.append(keep_copy(DKEY, dk_out, dk_hbm))
+            dk_ref[:, lanes(me)] = (grad * scale).astype(jnp.bfloat16)
         block_sum = jnp.sum(jnp.sum(dscores, axis=0, keepdims=True), axis=1, keepdims=True)
         bias_sums = bias_sums + jnp.where(spot == b, block_sum, 0.0)
     bias_out[...] = bias_sums
@@ -273,11 +281,11 @@
         grad = lax.dot_general(
             picked, k_all, (((0,), (0,)), ((), ())), preferred_element_type=jnp.float32
         )
-        dq_out[b] = (grad * scale).astype(jnp.bfloat16)
         if r < n - 1:
-            send(back_copy(DQUERY, dq_out, dq_hbm, b))
+            dq_out[b] = (grad * scale).astype(jnp.bfloat16)
+            send(back_copy(DQUERY, dq_out, dq_ref, b))
         else:
-            kept.append(keep_copy(DQUERY, dq_out, dq_hbm))
+            dq_ref[:, lanes(me)] = (grad * scale).astype(jnp.bfloat16)
 
     for r in range(1, ndp):
         other = lax.rem(here + r, ndp)
@@ -291,13 +299,24 @@
         ).wait_recv()
     db_ref[...] = jnp.sum(bias_in[...], axis=0)[:, : db_ref.shape[1]]
 
-    for kind, out in ((DVALUE, dv_hbm), (DKEY, dk_hbm), (DQUERY, dq_hbm)):
+    for kind, out in ((DVALUE, dv_ref), (DKEY, dk_ref), (DQUERY, dq_ref)):
         for r in range(n - 1):
             peer = peer_of(r)
-            wait_in(kind, out.at[0, :, lanes(peer)], peer)
+            wait_in(kind, out.at[:, lanes(peer)], peer)
     for copy in sent + bias_sent:
         copy.wait_send()
-    for copy in kept:
+
+
+def store_kernel(dq_ref, dk_ref, dv_ref, db_ref, dq_hbm, dk_hbm, dv_hbm, db_hbm, sem):
+    copies = [
+        pltpu.make_async_copy(dq_ref, dq_hbm.at[0], sem.at[0]),
+        pltpu.make_async_copy(dk_ref, dk_hbm.at[0], sem.at[1]),
+        pltpu.make_async_copy(dv_ref, dv_hbm.at[0], sem.at[2]),
+        pltpu.make_async_copy(db_ref, db_hbm, sem.at[3]),
+    ]
+    for copy in copies:
+        copy.start()
+    for copy in copies:
         copy.wait()
 
 
@@ -311,13 +330,14 @@
     padded = -(-n // 128) * 128
     half, full = jnp.bfloat16, jnp.float32
     any_ref = pl.BlockSpec(memory_space=pl.ANY)
-    smem = pl.BlockSpec(memory_space=pltpu.SMEM)
+    vmem = pl.BlockSpec(memory_space=pltpu.VMEM)
     field = jax.ShapeDtypeStruct(query.shape, query.dtype)
-    return pl.pallas_call(
+    held = pltpu.VMEM((rows, width), query.dtype)
+    grads = pl.pallas_call(
         functools.partial(kernel, n, ndp, head_dim),
-        out_shape=(field, field, field, jax.ShapeDtypeStruct((1, n), full)),
-        in_specs=[any_ref] * 5 + [smem] * 4,
-        out_specs=(any_ref, any_ref, any_ref, pl.BlockSpec(memory_space=pltpu.VMEM)),
+        out_shape=(held, held, held, pltpu.VMEM((1, n), full)),
+        in_specs=[any_ref] * 9,
+        out_specs=(vmem,) * 4,
         scratch_shapes=[
             pltpu.VMEM((n, rows, head_dim), half),
             pltpu.VMEM((n, rows, head_dim), half),
@@ -335,16 +355,28 @@
             pltpu.VMEM((n, rows, head_dim), half),
             pltpu.VMEM((1, padded), full),
             pltpu.VMEM((ndp, 1, padded), full),
+            pltpu.SMEM(score_bias.shape, full),
+            pltpu.SMEM(block_list.shape, jnp.int32),
+            pltpu.SMEM(block_count.shape, jnp.int32),
+            pltpu.SMEM(hit_count.shape, jnp.int32),
             pltpu.SemaphoreType.DMA((8, n)),
             pltpu.SemaphoreType.DMA((8, n)),
             pltpu.SemaphoreType.DMA((8,)),
             pltpu.SemaphoreType.DMA((ndp,)),
             pltpu.SemaphoreType.DMA((ndp,)),
+            pltpu.SemaphoreType.DMA((4,)),
         ],
         compiler_params=pltpu.CompilerParams(
             collective_id=0, has_side_effects=True, vmem_limit_bytes=60 * 1024 * 1024
         ),
     )(query, key, value, out_ctx, d_out, score_bias, block_list, block_count, hit_count)
+    return pl.pallas_call(
+        store_kernel,
+        out_shape=(field, field, field, jax.ShapeDtypeStruct((1, n), full)),
+        in_specs=[any_ref] * 4,
+        out_specs=(any_ref,) * 4,
+        scratch_shapes=[pltpu.SemaphoreType.DMA((4,))],
+    )(*(pltpu.with_memory_space_constraint(x, pltpu.VMEM) for x in grads))
 
 
 def solution(mesh):

time: 34.6 us -> 30.2 us (0.87)
  local copies, waits for them, and re-layouts: 3.73 us -> 0 us
  Pallas kernels: 29.4 us -> 28.8 us
    unnamed x10 -> x0, local copies, waits for them, and re-layouts: 3.73 us -> none
    pallas_call x1 -> x2, Pallas kernels: 29.4 us -> 28.8 us  [the longest x1 28 us: on_device(): pl.pallas_call(functools.partial(kernel, n, ndp, head_dim), out_shape=(he...]
where the time goes in v2:
time: 30.2 us; the launch traced here: 30.1 us
  Pallas kernels  28.8 us (95%)
  between operations  1.29 us (4%)
    pallas_call x1, Pallas kernels, on_device(): pl.pallas_call(functools.partial(kernel, n, ndp, head_dim), out_shape=(he...  28 us
    pallas_call x1, Pallas kernels, on_device(): pl.pallas_call(store_kernel, out_shape=(field, field, field, jax.ShapeDty...  0.78 us

profile of v2, /device:TPU:0, one launch (start us, length us, event | category | flops | bytes accessed | tf_op | source)
XLA Modules:
  0.0 30.1 jit_solution(5252739081019875800)
XLA Ops:
  1.3 28.0 %shard_map.120 = (bf16[128,512]{1,0:T(8,128)(2,1)S(1)}, bf16[128,512]{1,0:T(8,128)(2,1)S(1)}, bf16[128,512]{1,0:T(8,128)(2,1)S(1)}, f32[1,4]{1,0:T(1,128)S(1)}) custom-call(bf16[1,128,512]{2,1,0:T(8,128)(2,1)} %q_hbm.1, bf16[1,128,512]{2,1,0:T(8,128)(2,1)} %k_hbm.1, bf16[1,128,512]{2,1,0:T(8,128)(2,1)} %v_hbm.1, bf16[1,128,512]{2,1,0:T(8,128)(2,1)} %o_hbm.1, ...), custom_call_target="tpu_custom_call" | custom-call | tf_op jit(solution)/shard_map/pallas_call | solution.py:336
  29.3 0.8 %shard_map.121 = (bf16[1,128,512]{2,1,0:T(8,128)(2,1)}, bf16[1,128,512]{2,1,0:T(8,128)(2,1)}, bf16[1,128,512]{2,1,0:T(8,128)(2,1)}, f32[1,4]{1,0:T(1,128)}) custom-call(bf16[128,512]{1,0:T(8,128)(2,1)S(1)} %get-tuple-element.8.dq_ref, bf16[128,512]{1,0:T(8,128)(2,1)S(1)} %get-tuple-element.9.dk_ref, bf16[128,512]{1,0:T(8,128)(2,1)S(1)} %get-tuple-element.10.dv_ref, ...), custom_call_target="tpu_custom_call" | custom-call | tf_op jit(solution)/shard_map/pallas_call | solution.py:373

commit v3 on v2

v3 whole, which is shorter than its diff:
```python
import functools
import math

import jax
import jax.numpy as jnp
from jax import lax
from jax.experimental import pallas as pl
from jax.experimental.pallas import tpu as pltpu
from jax.sharding import PartitionSpec as P

MASKED = -1000000000.0
MESH = pl.DeviceIdType.MESH
KEY, QUERY, GRAD, VALUE, DELTA, DVALUE, DKEY, DQUERY, SHIFT, STATS, BIAS = range(11)


def kernel(
    n,
    ndp,
    head_dim,
    q_hbm,
    k_hbm,
    v_hbm,
    o_hbm,
    g_hbm,
    bias_hbm,
    list_hbm,
    count_hbm,
    hit_hbm,
    dq_ref,
    dk_ref,
    dv_ref,
    db_ref,
    kbuf,
    qbuf,
    gbuf,
    vbuf,
    delta_in,
    delta_out,
    g_own,
    o_own,
    probs,
    probs_half,
    ds_half,
    dv_out,
    dk_out,
    dq_out,
    bias_out,
    bias_in,
    shift_out,
    shift_in,
    stats_out,
    stats_in,
    dq_in,
    btot_out,
    btot_in,
    bias_ref,
    list_ref,
    count_ref,
    hit_ref,
    send_sem,
    recv_sem,
    own_sem,
    bias_send,
    bias_recv,
    table_sem,
):
    me = lax.axis_index("seq")
    here = lax.axis_index("dp")
    rows = q_hbm.shape[1]
    hits = n * rows
    slots = list_ref.shape[2]
    scale = 1.0 / math.sqrt(head_dim)
    above = n - 1 - me
    m = n // 2
    w, u = me % m, me // m
    wide = 2 * head_dim

    def peer_of(r):
        return jnp.where(r < above, n - 1 - r, r - above)

    def near_of(r):
        return u * m + (w + r) % m

    def lanes(z):
        return pl.ds(pl.multiple_of(z % m * wide, wide), wide)

    def slot(kind, z):
        return z if kind in (QUERY, GRAD) else z % m

    load_g = pltpu.make_async_copy(g_hbm.at[0], g_own, own_sem.at[DVALUE])
    load_o = pltpu.make_async_copy(o_hbm.at[0], o_own, own_sem.at[DKEY])
    load_g.start()
    load_o.start()
    tables = [
        pltpu.make_async_copy(src, dst, table_sem.at[i])
        for i, (src, dst) in enumerate(
            ((bias_hbm, bias_ref), (list_hbm, list_ref), (count_hbm, count_ref), (hit_hbm, hit_ref))
        )
    ]
    for copy in tables:
        copy.start()
    sources = {KEY: k_hbm, QUERY: q_hbm, GRAD: g_hbm, VALUE: v_hbm}
    targets = {KEY: kbuf, QUERY: qbuf, GRAD: gbuf, VALUE: vbuf}
    own = {}
    for kind in (KEY, QUERY, GRAD, VALUE):
        own[kind] = pltpu.make_async_copy(
            sources[kind].at[0, :, lanes(me)], targets[kind].at[slot(kind, me)], own_sem.at[kind]
        )
        own[kind].start()

    barrier = pltpu.get_barrier_semaphore()
    for r in range(n - 1):
        pl.semaphore_signal(barrier, inc=1, device_id={"seq": peer_of(r)}, device_id_type=MESH)
    for r in range(1, ndp):
        pl.semaphore_signal(
            barrier, inc=1, device_id={"dp": lax.rem(here + r, ndp)}, device_id_type=MESH
        )
    pl.semaphore_wait(barrier, n - 1 + ndp - 1)

    def out_copy(kind, peer):
        return pltpu.make_async_remote_copy(
            src_ref=sources[kind].at[0, :, lanes(peer)],
            dst_ref=targets[kind].at[slot(kind, me)],
            send_sem=send_sem.at[kind, peer],
            recv_sem=recv_sem.at[kind, me],
            device_id={"seq": peer},
            device_id_type=MESH,
        )

    def wait_in(kind, buf, peer):
        pltpu.make_async_remote_copy(
            src_ref=buf,
            dst_ref=buf,
            send_sem=send_sem.at[kind, peer],
            recv_sem=recv_sem.at[kind, peer],
            device_id={"seq": peer},
            device_id_type=MESH,
        ).wait_recv()

    sent = []

    def send(copy):
        copy.start()
        sent.append(copy)

    def peers(kind):
        if kind in (QUERY, GRAD):
            return [peer_of(r) for r in range(n - 1)]
        return [near_of(r) for r in range(1, m)]

    def push(kind, src, dst, peer):
        return pltpu.make_async_remote_copy(
            src_ref=src,
            dst_ref=dst,
            send_sem=send_sem.at[kind, peer],
            recv_sem=recv_sem.at[kind, me],
            device_id={"seq": peer},
            device_id_type=MESH,
        )

    for kind in (QUERY, KEY):
        for peer in peers(kind):
            send(out_copy(kind, peer))

    for copy in tables:
        copy.wait()
    hit_limit = hit_ref[0]
    lane = lax.broadcasted_iota(jnp.int32, (1, hits), 1)
    within = lax.broadcasted_iota(jnp.int32, (rows, 1), 0)

    def shift_step(b, carry):
        shift = jnp.full((1, hits), MASKED, jnp.float32)
        for qb in range(n):
            used = jnp.int32(0)
            for at in range(slots):
                hit = (list_ref[0, qb, at] == b) & (at < count_ref[0, qb])
                used = jnp.where(hit, jnp.int32(1), used)
            inside = (lane >= qb * rows) & (lane < (qb + 1) * rows)
            shift = jnp.where(inside & (used > 0), bias_ref[0, b], shift)
        shift_out[b // m, b % m] = shift
        return carry

    short = n <= 4
    lax.fori_loop(0, n, shift_step, 0, unroll=short)
    for half in range(2):
        taker = half * m + me // 2

        @pl.when(taker != me)
        def _(half=half, taker=taker):
            push(SHIFT, shift_out.at[half], shift_in.at[me % 2], taker).start()

        @pl.when(taker == me)
        def _(half=half):
            shift_in[me % 2] = shift_out[half]

    load_g.wait()
    load_o.wait()
    for h in range(n):
        cols = slice(h * head_dim, (h + 1) * head_dim)
        product = g_own[:, cols].astype(jnp.float32) * o_own[:, cols].astype(jnp.float32)
        delta_out[h // 2, h % 2] = jnp.sum(product.T, axis=0, keepdims=True)
    for r in range(n - 1):
        peer = peer_of(r)
        send(push(DELTA, delta_out.at[peer % m], delta_in.at[me], peer))
    delta_in[me] = delta_out[w]
    for kind in (GRAD, VALUE):
        for peer in peers(kind):
            send(out_copy(kind, peer))

    def arrive(kind):
        own[kind].wait()
        for peer in peers(kind):
            wait_in(kind, targets[kind].at[slot(kind, peer)], peer)

    arrive(KEY)
    arrive(QUERY)
    for i in range(2):
        head = 2 * w + i

        @pl.when(head != me)
        def _(i=i, head=head):
            wait_in(SHIFT, shift_in.at[i], head)

    def part(field, i):
        return field[..., i * head_dim : (i + 1) * head_dim]

    q_all = qbuf[...].reshape(hits, wide)
    tops = []
    for i in range(2):
        q_head = part(q_all, i)

        def score_step(b, top):
            real = jnp.where((u * m + b) * rows + within < hit_limit, 0.0, MASKED)
            scores = (
                lax.dot_general(
                    part(kbuf[b], i),
                    q_head,
                    (((1,), (1,)), ((), ())),
                    preferred_element_type=jnp.float32,
                )
                * scale
            )
            scores = (scores + shift_in[i, b]) + real
            probs[i, b] = scores
            return jnp.maximum(top, jnp.max(scores, axis=0, keepdims=True))

        top = lax.fori_loop(
            0, m, score_step, jnp.full((1, hits), -3e9, jnp.float32), unroll=short
        )

        def exp_step(b, total):
            raised = jnp.exp(probs[i, b] - top)
            probs[i, b] = raised
            return total + jnp.sum(raised, axis=0, keepdims=True)

        total = lax.fori_loop(0, m, exp_step, jnp.zeros((1, hits), jnp.float32), unroll=short)
        stats_out[i, 0] = top
        stats_out[i, 1] = total
        tops.append((top, total))
    across = (me + m) % n
    send(push(STATS, stats_out, stats_in, across))
    wait_in(STATS, stats_in, across)
    for i in range(2):
        top, total = tops[i]
        best = jnp.maximum(top, stats_in[i, 0])
        mine = jnp.exp(top - best)
        whole = total * mine + stats_in[i, 1] * jnp.exp(stats_in[i, 0] - best)
        factor = jnp.where(lane < hit_limit, mine / whole, 0.0)

        def scale_step(b, carry):
            scaled = probs[i, b] * factor
            probs[i, b] = scaled
            probs_half[i, b] = scaled.astype(jnp.bfloat16)
            return carry

        lax.fori_loop(0, m, scale_step, 0, unroll=short)

    arrive(GRAD)
    g_all = gbuf[...].reshape(hits, wide)
    for r in range(m):
        peer = near_of((r + 1) % m)
        b = peer % m
        for i in range(2):
            grad = jnp.dot(
                probs_half[i, b], part(g_all, i), preferred_element_type=jnp.float32
            )
            dv_out[b, :, i * head_dim : (i + 1) * head_dim] = grad.astype(jnp.bfloat16)
        if r < m - 1:
            send(push(DVALUE, dv_out.at[b], dv_ref.at[:, lanes(me)], peer))
        else:
            dv_ref[:, lanes(me)] = dv_out[b]

    for r in range(n - 1):
        peer = peer_of(r)
        wait_in(DELTA, delta_in.at[peer], peer)
    spot = lax.broadcasted_iota(jnp.int32, (1, bias_out.shape[2]), 1)
    sums = [jnp.zeros(spot.shape, jnp.float32) for _ in range(2)]
    arrive(VALUE)
    for r in range(m):
        peer = near_of((r + 1) % m)
        b = peer % m
        for i in range(2):
            delta = jnp.concatenate([delta_in[z, i] for z in range(n)], axis=1)
            dprobs = lax.dot_general(
                part(vbuf[b], i),
                part(g_all, i),
                (((1,), (1,)), ((), ())),
                preferred_element_type=jnp.float32,
            )
            dscores = probs[i, b] * (dprobs - delta)
            rounded = dscores.astype(jnp.bfloat16)
            ds_half[i, b] = rounded
            grad = jnp.dot(rounded, part(q_all, i), preferred_element_type=jnp.float32)
            dk_out[b, :, i * head_dim : (i + 1) * head_dim] = (grad * scale).astype(jnp.bfloat16)
            block_sum = jnp.sum(jnp.sum(dscores, axis=0, keepdims=True), axis=1, keepdims=True)
            sums[i] = sums[i] + jnp.where(spot == peer, block_sum, 0.0)
        if r < m - 1:
            send(push(DKEY, dk_out.at[b], dk_ref.at[:, lanes(me)], peer))
        else:
            dk_ref[:, lanes(me)] = dk_out[b]

    k_all = kbuf[...].reshape(m * rows, wide)
    for r in range(n):
        b = peer_of(r) if r < n - 1 else me
        for i in range(2):
            picked = ds_half[i, :, :, pl.ds(pl.multiple_of(b * rows, rows), rows)]
            grad = lax.dot_general(
                picked.reshape(m * rows, rows),
                part(k_all, i),
                (((0,), (0,)), ((), ())),
                preferred_element_type=jnp.float32,
            )
            dq_out[b, :, i * head_dim : (i + 1) * head_dim] = (grad * scale).astype(jnp.bfloat16)
        if r < n - 1:
            send(push(DQUERY, dq_out.at[b], dq_in.at[u, :, lanes(me)], b))
        else:
            dq_in[u, :, lanes(me)] = dq_out[b]

    for i in range(2):
        bias_out[i] = sums[i]
        bias_in[here, i] = sums[i]
    bias_sent = []
    for r in range(1, ndp):
        copy = pltpu.make_async_remote_copy(
            src_ref=bias_out,
            dst_ref=bias_in.at[here],
            send_sem=bias_send.at[r],
            recv_sem=bias_recv.at[here],
            device_id={"dp": lax.rem(here + r, ndp)},
            device_id_type=MESH,
        )
        copy.start()
        bias_sent.append(copy)
    for r in range(1, ndp):
        other = lax.rem(here + r, ndp)
        pltpu.make_async_remote_copy(
            src_ref=bias_in.at[other],
            dst_ref=bias_in.at[other],
            send_sem=bias_send.at[r],
            recv_sem=bias_recv.at[other],
            device_id={"dp": other},
            device_id_type=MESH,
        ).wait_recv()
    btot_out[...] = jnp.sum(bias_in[...], axis=0)
    for i in range(2):
        head = 2 * w + i

        @pl.when(head != me)
        def _(i=i, head=head):
            push(BIAS, btot_out.at[i], btot_in.at[u], head).start()

        @pl.when(head == me)
        def _(i=i):
            btot_in[u] = btot_out[i]

    for kind, out in ((DVALUE, dv_ref), (DKEY, dk_ref)):
        for peer in peers(kind):
            wait_in(kind, out.at[:, lanes(peer)], peer)
    for half in range(2):
        taker = half * m + me // 2

        @pl.when(taker != me)
        def _(half=half, taker=taker):
            push(SHIFT, shift_out.at[half], shift_in.at[me % 2], taker).wait_send()
            wait_in(BIAS, btot_in.at[half], taker)

    for i in range(2):
        head = 2 * w + i

        @pl.when(head != me)
        def _(i=i, head=head):
            push(BIAS, btot_out.at[i], btot_in.at[u], head).wait_send()

    db_ref[...] = (btot_in[0] + btot_in[1])[:, : db_ref.shape[1]]
    for r in range(n - 1):
        peer = peer_of(r)
        wait_in(DQUERY, dq_in.at[peer // m, :, lanes(peer)], peer)
    dq_ref[...] = (dq_in[0].astype(jnp.float32) + dq_in[1].astype(jnp.float32)).astype(
        jnp.bfloat16
    )
    for copy in sent + bias_sent:
        copy.wait_send()


def store_kernel(dq_ref, dk_ref, dv_ref, db_ref, dq_hbm, dk_hbm, dv_hbm, db_hbm, sem):
    copies = [
        pltpu.make_async_copy(dq_ref, dq_hbm.at[0], sem.at[0]),
        pltpu.make_async_copy(dk_ref, dk_hbm.at[0], sem.at[1]),
        pltpu.make_async_copy(dv_ref, dv_hbm.at[0], sem.at[2]),
        pltpu.make_async_copy(db_ref, db_hbm, sem.at[3]),
    ]
    for copy in copies:
        copy.start()
    for copy in copies:
        copy.wait()


def on_device(query, key, value, out_ctx, d_out, score_bias, block_list, block_count, hit_count):
    n = lax.axis_size("seq")
    ndp = lax.axis_size("dp")
    _, rows, width = query.shape
    head_dim = width // (score_bias.shape[0] * n)
    assert score_bias.shape[0] == 1 and block_list.shape[1] == n
    m, wide = n // 2, 2 * head_dim
    hits = n * rows
    padded = -(-n // 128) * 128
    half, full = jnp.bfloat16, jnp.float32
    any_ref = pl.BlockSpec(memory_space=pl.ANY)
    vmem = pl.BlockSpec(memory_space=pltpu.VMEM)
    field = jax.ShapeDtypeStruct(query.shape, query.dtype)
    held = pltpu.VMEM((rows, width), query.dtype)
    grads = pl.pallas_call(
        functools.partial(kernel, n, ndp, head_dim),
        out_shape=(held, held, held, pltpu.VMEM((1, n), full)),
        in_specs=[any_ref] * 9,
        out_specs=(vmem,) * 4,
        scratch_shapes=[
            pltpu.VMEM((m, rows, wide), half),
            pltpu.VMEM((n, rows, wide), half),
            pltpu.VMEM((n, rows, wide), half),
            pltpu.VMEM((m, rows, wide), half),
            pltpu.VMEM((n, 2, 1, rows), full),
            pltpu.VMEM((m, 2, 1, rows), full),
            pltpu.VMEM((rows, width), half),
            pltpu.VMEM((rows, width), half),
            pltpu.VMEM((2, m, rows, hits), full),
            pltpu.VMEM((2, m, rows, hits), half),
            pltpu.VMEM((2, m, rows, hits), half),
            pltpu.VMEM((m, rows, wide), half),
            pltpu.VMEM((m, rows, wide), half),
            pltpu.VMEM((n, rows, wide), half),
            pltpu.VMEM((2, 1, padded), full),
            pltpu.VMEM((ndp, 2, 1, padded), full),
            pltpu.VMEM((2, m, 1, hits), full),
            pltpu.VMEM((2, m, 1, hits), full),
            pltpu.VMEM((2, 2, 1, hits), full),
            pltpu.VMEM((2, 2, 1, hits), full),
            pltpu.VMEM((2, rows, width), half),
            pltpu.VMEM((2, 1, padded), full),
            pltpu.VMEM((2, 1, padded), full),
            pltpu.SMEM(score_bias.shape, full),
            pltpu.SMEM(block_list.shape, jnp.int32),
            pltpu.SMEM(block_count.shape, jnp.int32),
            pltpu.SMEM(hit_count.shape, jnp.int32),
            pltpu.SemaphoreType.DMA((11, n)),
            pltpu.SemaphoreType.DMA((11, n)),
            pltpu.SemaphoreType.DMA((8,)),
            pltpu.SemaphoreType.DMA((ndp,)),
            pltpu.SemaphoreType.DMA((ndp,)),
            pltpu.SemaphoreType.DMA((4,)),
        ],
        compiler_params=pltpu.CompilerParams(
            collective_id=0, has_side_effects=True, vmem_limit_bytes=60 * 1024 * 1024
        ),
    )(query, key, value, out_ctx, d_out, score_bias, block_list, block_count, hit_count)
    return pl.pallas_call(
        store_kernel,
        out_shape=(field, field, field, jax.ShapeDtypeStruct((1, n), full)),
        in_specs=[any_ref] * 4,
        out_specs=(any_ref,) * 4,
        scratch_shapes=[pltpu.SemaphoreType.DMA((4,))],
    )(*(pltpu.with_memory_space_constraint(x, pltpu.VMEM) for x in grads))


def solution(mesh):
    placed = (
        P("dp", "seq", None),
        P("dp", "seq", None),
        P("dp", "seq", None),
        P("dp", "seq", None),
        P("dp", "seq", None),
        P("seq", None),
        P("seq", None, None),
        P("seq", None),
        P("dp"),
    )
    return jax.shard_map(
        on_device,
        mesh=mesh,
        in_specs=placed,
        out_specs=(
            P("dp", "seq", None),
            P("dp", "seq", None),
            P("dp", "seq", None),
            P("seq", None),
        ),
        check_vma=False,
    )
```

time: 30.2 us -> 31.9 us (1.056)
  Pallas kernels: 28.8 us -> 30.5 us
    pallas_call x1, Pallas kernels: 28 us -> 29.7 us  [on_device(): pl.pallas_call(functools.partial(kernel, n, ndp, head_dim), out_shape=(he...]
where the time goes in v3:
time: 31.9 us; the launch traced here: 31.8 us
  Pallas kernels  30.5 us (96%)
  between operations  1.29 us (4%)
    pallas_call x1, Pallas kernels, on_device(): pl.pallas_call(functools.partial(kernel, n, ndp, head_dim), out_shape=(he...  29.7 us
    pallas_call x1, Pallas kernels, on_device(): pl.pallas_call(store_kernel, out_shape=(field, field, field, jax.ShapeDty...  0.78 us

profile of v3, /device:TPU:0, one launch (start us, length us, event | category | flops | bytes accessed | tf_op | source)
XLA Modules:
  0.0 31.8 jit_solution(15159105690770818683)
XLA Ops:
  1.3 29.7 %shard_map.120 = (bf16[128,512]{1,0:T(8,128)(2,1)S(1)}, bf16[128,512]{1,0:T(8,128)(2,1)S(1)}, bf16[128,512]{1,0:T(8,128)(2,1)S(1)}, f32[1,4]{1,0:T(1,128)S(1)}) custom-call(bf16[1,128,512]{2,1,0:T(8,128)(2,1)} %q_hbm.1, bf16[1,128,512]{2,1,0:T(8,128)(2,1)} %k_hbm.1, bf16[1,128,512]{2,1,0:T(8,128)(2,1)} %v_hbm.1, bf16[1,128,512]{2,1,0:T(8,128)(2,1)} %o_hbm.1, ...), custom_call_target="tpu_custom_call" | custom-call | tf_op jit(solution)/shard_map/pallas_call | solution.py:432
  31.0 0.8 %shard_map.121 = (bf16[1,128,512]{2,1,0:T(8,128)(2,1)}, bf16[1,128,512]{2,1,0:T(8,128)(2,1)}, bf16[1,128,512]{2,1,0:T(8,128)(2,1)}, f32[1,4]{1,0:T(1,128)}) custom-call(bf16[128,512]{1,0:T(8,128)(2,1)S(1)} %get-tuple-element.8.dq_ref, bf16[128,512]{1,0:T(8,128)(2,1)S(1)} %get-tuple-element.9.dk_ref, bf16[128,512]{1,0:T(8,128)(2,1)S(1)} %get-tuple-element.10.dv_ref, ...), custom_call_target="tpu_custom_call" | custom-call | tf_op jit(solution)/shard_map/pallas_call | solution.py:476
